TPU v7x, 256 devices: a whole 4x4x8 slice. The times are simulated.
256 devices in a mesh: dp: 32 (over x, y, core), tp: 8 (over z).
Axes of the slice: x: 4, y: 4, z: 8, core: 2. Of those that a mesh axis runs over, the one named last changes fastest.
Arguments:
- arrived_rows: bfloat16 [12288, 7168], P('dp', 'tp'), may hold values from -6 to 6
- row_counts: int32 [32], P('dp'), may hold values from 1 to 384, 4096 in all
- routes: int32 [4096, 8], P('dp'), may hold values from 0 to 31, all different within a row; in each aligned block of 128 rows (0 to 127, 128 to 255, ...) at most 40 rows name the same one
- gate_scale: float32 [4096, 8], P('dp'), may hold values from 0.1 to 0.6
- w_gate: bfloat16 [32, 7168, 1024], P('dp', 'tp'), may hold values from -0.0625 to 0.0625
- w_up: bfloat16 [32, 7168, 1024], P('dp', 'tp'), may hold values from -0.0625 to 0.0625
- w_down: bfloat16 [32, 1024, 7168], P('dp', None, 'tp'), may hold values from -0.1875 to 0.1875
- cotangent: bfloat16 [4096, 7168], P('dp', 'tp'), may hold values from -6 to 6
Outputs:
- layer_out: bfloat16 [4096, 7168], P('dp', 'tp')
- grad_rows: bfloat16 [12288, 7168], P('dp', 'tp')
Inputs may be any that keep to these rules, and one draw needn't show every extreme that they name: `row_counts`: the counts sum to exactly 4096; the largest is exactly 384. `routes`: each row names 8 different experts; within the 128 rows of one index of dp no expert is named by more than 40 rows, a bound that some block reaches.
All inputs are finite; a program needn't handle non-finite values. No bound on the sum of `row_counts` on one device may be relied on, other than what follows from the above.
Results may differ from a plain program's by a relative error of at most 0.03.
Values may be sent and summed in bfloat16 or wider, within the bound.
No kernel may reach another device: no remote copies, remote signals or barrier semaphores. Data moves between devices by JAX's collectives and lax.ppermute only.
A program may use at most 64 MiB of HBM per device.

v0:
```python
import jax
import jax.numpy as jnp
from jax import lax
from jax.sharding import PartitionSpec as P

BF = jnp.bfloat16
F32 = jnp.float32


def rounded(tensor):
    return lax.optimization_barrier(tensor.astype(BF))


def select(left, right):
    return jnp.dot(left, right, preferred_element_type=F32).astype(BF)


def select_t(left, right):
    return lax.dot_general(
        left, right, (((0,), (0,)), ((), ())), preferred_element_type=F32
    ).astype(BF)


def dot_nt(left, right):
    return lax.dot_general(left, right, (((1,), (1,)), ((), ())), preferred_element_type=F32)


def on_device(arrived_rows, row_counts, routes, gate_scale, w_gate, w_up, w_down, cotangent):
    members = lax.axis_size("dp")
    myself = lax.axis_index("dp")
    slot_count, part = arrived_rows.shape
    rows, top = routes.shape
    capacity = rows * top // members + rows * top // (4 * members)
    per_peer = -(-(slot_count // members) // 16) * 16
    gate_proj, up_proj, down_proj = (w_gate[0], w_up[0], w_down[0])

    def exchange(tensor):
        return lax.all_to_all(tensor, "dp", split_axis=0, concat_axis=0, tiled=True)

    ids = jnp.arange(members, dtype=jnp.int32)
    chosen = routes.T[None, :, :] == ids[:, None, None]
    named = jnp.any(chosen, axis=1)
    before = jnp.arange(rows)[:, None] < jnp.arange(rows)[None, :]
    place = jnp.dot(named.astype(BF), before.astype(BF), preferred_element_type=F32)
    place = jnp.where(named, place.astype(jnp.int32), -1)
    slots = jnp.arange(capacity, dtype=jnp.int32)
    hot = place[:, None, :] == slots[None, :, None]
    pack = hot.astype(BF).reshape(members * capacity, rows)
    shipped_grad = exchange(select(pack, cotangent).reshape(members, capacity, part))
    all_counts = lax.all_gather(row_counts, "dp", axis=0, tiled=True)
    starts = jnp.sum(jnp.where(ids[None, :] < ids[:, None], all_counts[None, :], 0), axis=1)
    my_start = starts[myself]
    my_count = all_counts[myself]
    column = jnp.arange(per_peer, dtype=jnp.int32)
    source_slot = (ids[:, None] - my_start) % members + column[None, :] * members
    source_slot = jnp.where(source_slot < my_count, source_slot, -1).reshape(-1)
    spread = (source_slot[:, None] == jnp.arange(slot_count, dtype=jnp.int32)[None, :]).astype(BF)
    incoming = exchange(select(spread, arrived_rows).reshape(members, per_peer, part))
    offset = (jnp.arange(rows, dtype=jnp.int32) * members + myself)[:, None] - starts[None, :]
    held = (offset >= 0) & (offset < all_counts[None, :])
    taken = jnp.where(held, offset // members, -1)
    take = (taken[:, :, None] == column[None, None, :]).astype(BF).reshape(rows, -1)
    balanced = select(take, incoming.reshape(-1, part))
    shipped = exchange(select(pack, balanced).reshape(members, capacity, part))
    grad_part = rounded(dot_nt(shipped_grad.reshape(-1, part), down_proj))
    hidden_grad = lax.psum_scatter(grad_part, "tp", scatter_dimension=0, tiled=True)
    flat = shipped.reshape(-1, part)
    gate_part = rounded(jnp.dot(flat, gate_proj, preferred_element_type=F32))
    up_part = rounded(jnp.dot(flat, up_proj, preferred_element_type=F32))
    gate_pre = lax.psum_scatter(gate_part, "tp", scatter_dimension=0, tiled=True)
    up_pre = lax.psum_scatter(up_part, "tp", scatter_dimension=0, tiled=True)
    gate_pre, up_pre, hidden_grad = (v.astype(F32) for v in (gate_pre, up_pre, hidden_grad))
    sigmoid_gate = jax.nn.sigmoid(gate_pre)
    hidden = (gate_pre * sigmoid_gate * up_pre).astype(BF)
    gate_grad = (
        hidden_grad * up_pre * sigmoid_gate * (1.0 + gate_pre * (1.0 - sigmoid_gate))
    ).astype(BF)
    up_grad = (hidden_grad * gate_pre * sigmoid_gate).astype(BF)
    gate_grad = lax.all_gather(gate_grad, "tp", axis=0, tiled=True)
    up_grad = lax.all_gather(up_grad, "tp", axis=0, tiled=True)
    hidden = lax.all_gather(hidden, "tp", axis=0, tiled=True)
    scale_high = lax.optimization_barrier(gate_scale.astype(BF))
    scale_low = (gate_scale - scale_high.astype(F32)).astype(BF)

    def weights(scale):
        per_expert = jnp.sum(jnp.where(chosen, scale.astype(F32).T[None], 0.0), axis=1)
        return jnp.where(hot, per_expert[:, None, :], 0.0).astype(BF).reshape(-1, rows)

    mix = jnp.concatenate([weights(scale_high), weights(scale_low)], axis=1)

    def combine(returned):
        both = lax.dot_general(
            mix, returned.reshape(-1, part), (((0,), (0,)), ((), ())), preferred_element_type=F32
        )
        return (both[:rows] + both[rows:]).astype(BF)

    input_grad = (dot_nt(gate_grad, gate_proj) + dot_nt(up_grad, up_proj)).astype(BF)
    returned_grad = exchange(input_grad.reshape(members, capacity, part))
    expert_out = jnp.dot(hidden, down_proj, preferred_element_type=F32).astype(BF)
    returned_out = exchange(expert_out.reshape(members, capacity, part))
    balanced_grad = combine(returned_grad)
    leaving = select_t(take, balanced_grad)
    arriving = exchange(leaving.reshape(members, per_peer, part))
    grad_rows = select_t(spread, arriving.reshape(-1, part))
    layer_out = combine(returned_out)
    return (layer_out, grad_rows)


def solution(mesh):
    placed = (
        P("dp", "tp"),
        P("dp"),
        P("dp", None),
        P("dp", None),
        P("dp", "tp", None),
        P("dp", "tp", None),
        P("dp", None, "tp"),
        P("dp", "tp"),
    )
    return jax.shard_map(
        on_device,
        mesh=mesh,
        in_specs=placed,
        out_specs=(P("dp", "tp"), P("dp", "tp")),
        check_vma=False,
    )
```

profile of v0, /device:TPU:1, one launch (start us, length us, event | category | flops | bytes accessed | tf_op | source)
XLA Modules:
  0.0 430.1 jit_solution(9517103195963572123)
XLA Ops:
  7.2 0.9 fusion.30
  8.6 1.7 convolution_convert_fusion.4
  10.3 39.3 %all_to_all.30 = bf16[32,40,896]{2,1,0:T(8,128)(2,1)S(1)} all-to-all(bf16[32,40,896]{2,1,0:T(8,128)(2,1)S(1)} %bitcast.73), channel_id=1, replica_groups=mesh['dp'=32,'tp'=8] {'dp'}, dimensions={0} | all-to-all | bytes 4587520 | tf_op jit(solution)/shard_map/all_to_all | solution.py:38
  49.6 4.3 convolution_convert_fusion
  55.2 0.8 dynamic-update-slice
  56.0 10.0 %all-reduce = s32[32]{0:T(128)S(1)} all-reduce(s32[32]{0:T(128)S(1)} %dynamic-update-slice), channel_id=1, replica_groups=mesh['dp'=32,'tp'=8] {'dp'}, use_global_device_ids=true, to_apply=%add | all-reduce | flops 32 | bytes 256
  68.8 1.6 convolution_convert_fusion.7
  70.4 8.7 %all-to-all-start = ((bf16[32,16,896]{2,1,0:T(8,128)(2,1)}), bf16[32,16,896]{2,1,0:T(8,128)(2,1)S(1)}, u32[]{:S(2)}, u32[]{:S(2)}) async-start(bf16[32,16,896]{2,1,0:T(8,128)(2,1)} %bitcast.80), calls=%async_computation | async-start | bytes 1835008 | tf_op jit(solution)/shard_map/all_to_all | solution.py:38
  79.3 15.3 %all-to-all-done = bf16[32,16,896]{2,1,0:T(8,128)(2,1)S(1)} async-done(((bf16[32,16,896]{2,1,0:T(8,128)(2,1)}), bf16[32,16,896]{2,1,0:T(8,128)(2,1)S(1)}, u32[]{:S(2)}, u32[]{:S(2)}) %all-to-all-start) | async-done | bytes 917536 | tf_op jit(solution)/shard_map/all_to_all | solution.py:38
  94.6 2.5 convolution_convert_fusion.5
  97.1 34.8 %all_to_all.31 = bf16[32,40,896]{2,1,0:T(8,128)(2,1)S(1)} all-to-all(bf16[32,40,896]{2,1,0:T(8,128)(2,1)} %bitcast.72), channel_id=1, replica_groups=mesh['dp'=32,'tp'=8] {'dp'}, dimensions={0} | all-to-all | bytes 4587520 | tf_op jit(solution)/shard_map/all_to_all | solution.py:38
  131.9 1.4 copy-done.1
  133.3 4.1 convolution_convert_fusion.2
  137.5 6.6 %convolution_convert_fusion.1 = bf16[1280,1024]{1,0:T(8,128)(2,1)} fusion(bf16[1280,896]{1,0:T(8,128)(2,1)} %bitcast.76, bf16[1,896,1024]{2,1,0:T(8,128)(2,1)} %param.13), kind=kOutput, calls=%fused_computation.2 | convolution fusion | flops 2350120960 | bytes 6750208 | tf_op jit(solution)/shard_map/dot_general | solution.py:69
  144.2 32.4 %reduce-scatter.4.cloned.1.call-done = bf16[160,1024]{1,0:T(8,128)(2,1)} async-done(((bf16[1280,1024]{1,0:T(8,128)(2,1)}), bf16[160,1024]{1,0:T(8,128)(2,1)}) %reduce-scatter.4.cloned.1.call-update) | async-done | bytes 327696 | tf_op jit(solution)/shard_map/reduce_scatter | solution.py:70
  176.5 46.1 %reduce-scatter.6.cloned.1.call-done = bf16[160,1024]{1,0:T(8,128)(2,1)} async-done(((bf16[1280,1024]{1,0:T(8,128)(2,1)}), bf16[160,1024]{1,0:T(8,128)(2,1)}) %reduce-scatter.6.cloned.1.call-update) | async-done | bytes 327696 | tf_op jit(solution)/shard_map/reduce_scatter | solution.py:71
  222.6 2.5 fusion.18
  226.4 41.7 %all-gather.6.cloned.1.call-done = bf16[1280,1024]{1,0:T(8,128)(2,1)} async-done(((bf16[160,1024]{1,0:T(8,128)(2,1)}), bf16[1280,1024]{1,0:T(8,128)(2,1)}) %all-gather.6.cloned.1.call-update) | async-done | bytes 2621456 | tf_op jit(solution)/shard_map/all_gather | solution.py:79
  268.1 6.7 %fusion.4 = f32[1280,896]{1,0:T(8,128)} fusion(bf16[1280,1024]{1,0:T(8,128)(2,1)} %all-gather.6.cloned.1.call-done, bf16[1,896,1024]{2,1,0:T(8,128)(2,1)S(1)} %copy-done), kind=kOutput, calls=%fused_computation.11 | convolution fusion | flops 2348810240 | bytes 9043968 | tf_op jit(solution)/shard_map/dot_general | solution.py:25
  274.8 36.4 %all-gather.8.cloned.1.call-done = bf16[1280,1024]{1,0:T(8,128)(2,1)} async-done(((bf16[160,1024]{1,0:T(8,128)(2,1)}), bf16[1280,1024]{1,0:T(8,128)(2,1)}) %all-gather.8.cloned.1.call-update) | async-done | bytes 2621456 | tf_op jit(solution)/shard_map/all_gather | solution.py:80
  311.3 7.9 %add_convert_fusion = bf16[1280,896]{1,0:T(8,128)(2,1)} fusion(f32[1280,896]{1,0:T(8,128)} %fusion.4, bf16[1280,1024]{1,0:T(8,128)(2,1)} %all-gather.8.cloned.1.call-done, bf16[1,896,1024]{2,1,0:T(8,128)(2,1)} %param.13), kind=kOutput, calls=%fused_computation | convolution fusion | flops 2351104000 | bytes 11337728 | tf_op jit(solution)/shard_map/dot_general | solution.py:25
  319.2 10.5 %all-to-all-start.4 = ((bf16[32,40,896]{2,1,0:T(8,128)(2,1)}), bf16[32,40,896]{2,1,0:T(8,128)(2,1)}, u32[]{:S(2)}, u32[]{:S(2)}) async-start(bf16[32,40,896]{2,1,0:T(8,128)(2,1)} %bitcast.77), calls=%async_computation.7 | async-start | bytes 4587520 | tf_op jit(solution)/shard_map/all_to_all | solution.py:38
  329.7 24.2 %all-gather.4.cloned.1.call-done = bf16[1280,1024]{1,0:T(8,128)(2,1)} async-done(((bf16[160,1024]{1,0:T(8,128)(2,1)}), bf16[1280,1024]{1,0:T(8,128)(2,1)}) %all-gather.4.cloned.1.call-update) | async-done | bytes 2621456 | tf_op jit(solution)/shard_map/all_gather | solution.py:81
  353.9 6.6 %convolution_convert_fusion.3 = bf16[1280,896]{1,0:T(8,128)(2,1)} fusion(bf16[1280,1024]{1,0:T(8,128)(2,1)} %all-gather.4.cloned.1.call-done, bf16[1,1024,896]{2,1,0:T(8,128)(2,1)} %param.14), kind=kOutput, calls=%fused_computation.4 | convolution fusion | flops 2349957120 | bytes 6750208 | tf_op jit(solution)/shard_map/dot_general | solution.py:99
  360.5 10.7 %all-to-all-start.2 = ((bf16[32,40,896]{2,1,0:T(8,128)(2,1)}), bf16[32,40,896]{2,1,0:T(8,128)(2,1)}, u32[]{:S(2)}, u32[]{:S(2)}) async-start(bf16[32,40,896]{2,1,0:T(8,128)(2,1)} %bitcast.74), calls=%async_computation.4 | async-start | bytes 4587520 | tf_op jit(solution)/shard_map/all_to_all | solution.py:38
  371.8 2.5 fusion.23
  374.3 1.4 convolution_convert_fusion.6
  375.7 26.0 %all-to-all-done.2 = bf16[32,40,896]{2,1,0:T(8,128)(2,1)} async-done(((bf16[32,40,896]{2,1,0:T(8,128)(2,1)}), bf16[32,40,896]{2,1,0:T(8,128)(2,1)}, u32[]{:S(2)}, u32[]{:S(2)}) %all-to-all-start.2) | async-done | bytes 2293792 | tf_op jit(solution)/shard_map/all_to_all | solution.py:38
  401.6 4.5 %all-to-all-start.5 = ((bf16[32,16,896]{2,1,0:T(8,128)(2,1)}), bf16[32,16,896]{2,1,0:T(8,128)(2,1)S(1)}, u32[]{:S(2)}, u32[]{:S(2)}) async-start(bf16[32,16,896]{2,1,0:T(8,128)(2,1)} %bitcast.23), calls=%async_computation.8 | async-start | bytes 1835008 | tf_op jit(solution)/shard_map/all_to_all | solution.py:38
  406.1 2.5 fusion.24
  409.4 12.3 %all-to-all-done.5 = bf16[32,16,896]{2,1,0:T(8,128)(2,1)S(1)} async-done(((bf16[32,16,896]{2,1,0:T(8,128)(2,1)}), bf16[32,16,896]{2,1,0:T(8,128)(2,1)S(1)}, u32[]{:S(2)}, u32[]{:S(2)}) %all-to-all-start.5) | async-done | bytes 917536 | tf_op jit(solution)/shard_map/all_to_all | solution.py:38
  421.7 1.5 convolution_convert_fusion.8
  (52 shorter events, 6.6 us)
Async XLA Ops:
  7.2 126.1 %copy-start = (bf16[1,896,1024]{2,1,0:T(8,128)(2,1)S(1)}, bf16[1,896,1024]{2,1,0:T(8,128)(2,1)}, u32[]{:S(2)}) copy-start(bf16[1,896,1024]{2,1,0:T(8,128)(2,1)} %param.12) | copy-start | bytes 5505028
  7.2 137.0 %reduce-scatter.8.cloned.1.call-start = ((), (), s32[]{:S(2)}) async-start(), calls=%async_computation.12 | async-start | bytes 2949120 | tf_op jit(solution)/shard_map/reduce_scatter | solution.py:66
  10.3 39.3 %copy-start.4 = (bf16[1,1024,896]{2,1,0:T(8,128)(2,1)S(1)}, bf16[1,1024,896]{2,1,0:T(8,128)(2,1)}, u32[]{:S(2)}) copy-start(bf16[1,1024,896]{2,1,0:T(8,128)(2,1)} %param.14) | copy-start | bytes 5505028
  53.9 0.7 copy-start.6
  53.9 14.9 %copy-start.5 = (bf16[384,896]{1,0:T(8,128)(2,1)S(1)}, bf16[384,896]{1,0:T(8,128)(2,1)}, u32[]{:S(2)}) copy-start(bf16[384,896]{1,0:T(8,128)(2,1)} %param.8) | copy-start | bytes 2064388
  70.4 24.2 %all-to-all-start = ((bf16[32,16,896]{2,1,0:T(8,128)(2,1)}), bf16[32,16,896]{2,1,0:T(8,128)(2,1)S(1)}, u32[]{:S(2)}, u32[]{:S(2)}) async-start(bf16[32,16,896]{2,1,0:T(8,128)(2,1)} %bitcast.80), calls=%async_computation | async-start | bytes 1835008 | tf_op jit(solution)/shard_map/all_to_all | solution.py:38
  79.1 97.4 %reduce-scatter.4.cloned.1.call-start = ((), (), s32[]{:S(2)}) async-start(), calls=%async_computation.9 | async-start | bytes 2949120 | tf_op jit(solution)/shard_map/reduce_scatter | solution.py:70
  131.9 1.4 copy-start.1
  137.5 85.2 %reduce-scatter.6.cloned.1.call-start = ((), (), s32[]{:S(2)}) async-start(), calls=%async_computation.10 | async-start | bytes 2949120 | tf_op jit(solution)/shard_map/reduce_scatter | solution.py:71
  144.1 124.0 %all-gather.6.cloned.1.call-start = ((), (), s32[]{:S(2)}) async-start(), calls=%async_computation.13 | async-start | bytes 2949120 | tf_op jit(solution)/shard_map/all_gather | solution.py:79
  225.2 86.0 %all-gather.8.cloned.1.call-start = ((), (), s32[]{:S(2)}) async-start(), calls=%async_computation.14 | async-start | bytes 2949120 | tf_op jit(solution)/shard_map/all_gather | solution.py:80
  225.8 128.1 %all-gather.4.cloned.1.call-start = ((), (), s32[]{:S(2)}) async-start(), calls=%async_computation.11 | async-start | bytes 2949120 | tf_op jit(solution)/shard_map/all_gather | solution.py:81
  319.2 41.3 %all-to-all-start.4 = ((bf16[32,40,896]{2,1,0:T(8,128)(2,1)}), bf16[32,40,896]{2,1,0:T(8,128)(2,1)}, u32[]{:S(2)}, u32[]{:S(2)}) async-start(bf16[32,40,896]{2,1,0:T(8,128)(2,1)} %bitcast.77), calls=%async_computation.7 | async-start | bytes 4587520 | tf_op jit(solution)/shard_map/all_to_all | solution.py:38
  360.5 10.7 %copy-start.3 = (f32[128,8]{0,1:T(8,128)S(1)}, f32[128,8]{0,1:T(8,128)}, u32[]{:S(2)}) copy-start(f32[128,8]{0,1:T(8,128)} %param.11) | copy-start | bytes 12292
  360.5 11.0 %copy-start.2 = (s32[128,8]{0,1:T(8,128)S(1)}, s32[128,8]{0,1:T(8,128)}, u32[]{:S(2)}) copy-start(s32[128,8]{0,1:T(8,128)} %param.10) | copy-start | bytes 12292
  360.5 41.1 %all-to-all-start.2 = ((bf16[32,40,896]{2,1,0:T(8,128)(2,1)}), bf16[32,40,896]{2,1,0:T(8,128)(2,1)}, u32[]{:S(2)}, u32[]{:S(2)}) async-start(bf16[32,40,896]{2,1,0:T(8,128)(2,1)} %bitcast.74), calls=%async_computation.4 | async-start | bytes 4587520 | tf_op jit(solution)/shard_map/all_to_all | solution.py:38
  401.6 20.1 %all-to-all-start.5 = ((bf16[32,16,896]{2,1,0:T(8,128)(2,1)}), bf16[32,16,896]{2,1,0:T(8,128)(2,1)S(1)}, u32[]{:S(2)}, u32[]{:S(2)}) async-start(bf16[32,16,896]{2,1,0:T(8,128)(2,1)} %bitcast.23), calls=%async_computation.8 | async-start | bytes 1835008 | tf_op jit(solution)/shard_map/all_to_all | solution.py:38
Sparse Core Ops, SparseCore 0:
  54.0 39.0 reduce-scatter.7
  137.6 38.9 reduce-scatter.3
  179.1 43.4 reduce-scatter.5
  225.3 42.7 all-gather.5
  270.3 40.9 all-gather.7
  312.9 40.9 all-gather.3
where the time goes:
time: 431 us; the launch traced here: 430 us
  waiting for transfers between devices  235 us (55%)
  blocking collectives  84.1 us (20%)
  matrix products  50.1 us (12%)
  starting transfers between devices  34.8 us (8%)
  between operations  15 us (3%)
  other arithmetic  6.42 us (1%)
    all_to_all x2, blocking collectives, exchange(): return lax.all_to_all(tensor, 'dp', split_axis=0, concat_axis=0, tiled=True)  74.1 us
    all_to_all x4, waiting for transfers between devices, exchange(): return lax.all_to_all(tensor, 'dp', split_axis=0, concat_axis=0, tiled=True)  53.6 us
    reduce_scatter x1, waiting for transfers between devices, on_device(): up_pre = lax.psum_scatter(up_part, 'tp', scatter_dimension=0, tiled=True)  46.1 us
    all_gather x1, waiting for transfers between devices, on_device(): gate_grad = lax.all_gather(gate_grad, 'tp', axis=0, tiled=True)  41.7 us
    all_gather x1, waiting for transfers between devices, on_device(): up_grad = lax.all_gather(up_grad, 'tp', axis=0, tiled=True)  36.4 us
    all_to_all x4, starting transfers between devices, exchange(): return lax.all_to_all(tensor, 'dp', split_axis=0, concat_axis=0, tiled=True)  34.3 us
    reduce_scatter x1, waiting for transfers between devices, on_device(): lax.psum_scatter(gate_part, 'tp', scatter_dimension=0, tiled=True)  32.4 us
    all_gather x1, waiting for transfers between devices, on_device(): hidden = lax.all_gather(hidden, 'tp', axis=0, tiled=True)  24.2 us
  transfers between devices with their start and end apart: 10, of which 8 were waited for; matrix products, arithmetic and copies ran while one was open for 11% of the time, Pallas kernels for 0%

commit v1 on v0

--- a/solution.py
+++ b/solution.py
@@ -2,6 +2,7 @@
 import jax.numpy as jnp
 from jax import lax
 from jax.sharding import PartitionSpec as P
+from jax.lax import all_gather
 
 BF = jnp.bfloat16
 F32 = jnp.float32
@@ -77,8 +78,15 @@
     ).astype(BF)
     up_grad = (hidden_grad * gate_pre * sigmoid_gate).astype(BF)
     gate_grad = lax.all_gather(gate_grad, "tp", axis=0, tiled=True)
-    up_grad = lax.all_gather(up_grad, "tp", axis=0, tiled=True)
-    hidden = lax.all_gather(hidden, "tp", axis=0, tiled=True)
+
+    def match_zones_now(patch, buf, chip_axis):
+        return jnp.split(
+            all_gather(jnp.concatenate([patch, buf], axis=1), chip_axis, tiled=True, axis=0),
+            [patch.shape[1]],
+            axis=1,
+        )
+
+    up_grad, hidden = match_zones_now(up_grad, hidden, "tp")
     scale_high = lax.optimization_barrier(gate_scale.astype(BF))
     scale_low = (gate_scale - scale_high.astype(F32)).astype(BF)
 

time: 431 us -> 447 us (1.037)
  waiting for transfers between devices: 235 us -> 260 us
  starting transfers between devices: 34.8 us -> 26.6 us
    all_to_all x4, waiting for transfers between devices: 53.6 us -> 77.6 us  [exchange(): return lax.all_to_all(tensor, 'dp', split_axis=0, concat_axis=0, tiled=True)]
    all_to_all x4, starting transfers between devices: 34.3 us -> 26.2 us  [exchange(): return lax.all_to_all(tensor, 'dp', split_axis=0, concat_axis=0, tiled=True)]
    all_gather x2 -> x1, waiting for transfers between devices: 60.6 us -> 61.7 us  [match_zones_now(): all_gather(jnp.concatenate([patch, buf], axis=1), chip_axis, tiled=True,...]
  transfers between devices with their start and end apart: 10 -> 9, of which waited for: 8 -> 8; matrix products, arithmetic and copies ran while one was open for 11% -> 9% of each run, Pallas kernels for 0% -> 0%
where the time goes in v1:
time: 447 us
  waiting for transfers between devices  260 us (58%)
  blocking collectives  84.2 us (19%)
  matrix products  50.1 us (11%)
  starting transfers between devices  26.6 us (6%)
  between operations  14.7 us (3%)
  other arithmetic  7.14 us (2%)
    all_to_all x4, waiting for transfers between devices, exchange(): return lax.all_to_all(tensor, 'dp', split_axis=0, concat_axis=0, tiled=True)  77.6 us
    all_to_all x2, blocking collectives, exchange(): return lax.all_to_all(tensor, 'dp', split_axis=0, concat_axis=0, tiled=True)  74.1 us
    all_gather x1, waiting for transfers between devices, match_zones_now(): all_gather(jnp.concatenate([patch, buf], axis=1), chip_axis, tiled=True,...  61.7 us
    reduce_scatter x1, waiting for transfers between devices, on_device(): up_pre = lax.psum_scatter(up_part, 'tp', scatter_dimension=0, tiled=True)  46 us
    all_gather x1, waiting for transfers between devices, on_device(): gate_grad = lax.all_gather(gate_grad, 'tp', axis=0, tiled=True)  41.8 us
    reduce_scatter x1, waiting for transfers between devices, on_device(): lax.psum_scatter(gate_part, 'tp', scatter_dimension=0, tiled=True)  32.4 us
    all_to_all x4, starting transfers between devices, exchange(): return lax.all_to_all(tensor, 'dp', split_axis=0, concat_axis=0, tiled=True)  26.2 us
    dot_general x3, matrix products, dot_nt(): lax.dot_general(left, right, (((1,), (1,)), ((), ())), preferred_element_...  19.1 us
  transfers between devices with their start and end apart: 9, of which 8 were waited for; matrix products, arithmetic and copies ran while one was open for 9% of the time, Pallas kernels for 0%

profile of v1, /device:TPU:1, one launch (start us, length us, event | category | flops | bytes accessed | tf_op | source)
XLA Modules:
  0.0 446.5 jit_solution(14766364241612112263)
XLA Ops:
  7.2 0.9 fusion.32
  8.6 1.7 convolution_convert_fusion.5
  10.3 39.3 %all_to_all.30 = bf16[32,40,896]{2,1,0:T(8,128)(2,1)S(1)} all-to-all(bf16[32,40,896]{2,1,0:T(8,128)(2,1)S(1)} %bitcast.71), channel_id=1, replica_groups=mesh['dp'=32,'tp'=8] {'dp'}, dimensions={0} | all-to-all | bytes 4587520 | tf_op jit(solution)/shard_map/all_to_all | solution.py:39
  49.6 4.3 convolution_convert_fusion.2
  56.0 10.0 %all-reduce = s32[32]{0:T(128)S(1)} all-reduce(s32[32]{0:T(128)S(1)} %dynamic-update-slice), channel_id=1, replica_groups=mesh['dp'=32,'tp'=8] {'dp'}, use_global_device_ids=true, to_apply=%add | all-reduce | flops 32 | bytes 256
  68.8 1.6 convolution_convert_fusion.7
  70.5 8.7 %all-to-all-start.1 = ((bf16[32,16,896]{2,1,0:T(8,128)(2,1)}), bf16[32,16,896]{2,1,0:T(8,128)(2,1)S(1)}, u32[]{:S(2)}, u32[]{:S(2)}) async-start(bf16[32,16,896]{2,1,0:T(8,128)(2,1)} %bitcast.78), calls=%async_computation.2 | async-start | bytes 1835008 | tf_op jit(solution)/shard_map/all_to_all | solution.py:39
  79.3 15.3 %all-to-all-done.1 = bf16[32,16,896]{2,1,0:T(8,128)(2,1)S(1)} async-done(((bf16[32,16,896]{2,1,0:T(8,128)(2,1)}), bf16[32,16,896]{2,1,0:T(8,128)(2,1)S(1)}, u32[]{:S(2)}, u32[]{:S(2)}) %all-to-all-start.1) | async-done | bytes 917536 | tf_op jit(solution)/shard_map/all_to_all | solution.py:39
  94.6 2.5 convolution_convert_fusion.4
  97.1 34.8 %all_to_all.31 = bf16[32,40,896]{2,1,0:T(8,128)(2,1)S(1)} all-to-all(bf16[32,40,896]{2,1,0:T(8,128)(2,1)} %bitcast.70), channel_id=1, replica_groups=mesh['dp'=32,'tp'=8] {'dp'}, dimensions={0} | all-to-all | bytes 4587520 | tf_op jit(solution)/shard_map/all_to_all | solution.py:39
  131.9 1.5 copy-done.1
  133.3 4.1 convolution_convert_fusion.1
  137.5 6.6 %convolution_convert_fusion = bf16[1280,1024]{1,0:T(8,128)(2,1)} fusion(bf16[1280,896]{1,0:T(8,128)(2,1)} %bitcast.74, bf16[1,896,1024]{2,1,0:T(8,128)(2,1)} %param.13), kind=kOutput, calls=%fused_computation.1 | convolution fusion | flops 2350120960 | bytes 6750208 | tf_op jit(solution)/shard_map/dot_general | solution.py:70
  144.2 32.4 %reduce-scatter.6.cloned.1.call-done = bf16[160,1024]{1,0:T(8,128)(2,1)} async-done(((bf16[1280,1024]{1,0:T(8,128)(2,1)}), bf16[160,1024]{1,0:T(8,128)(2,1)}) %reduce-scatter.6.cloned.1.call-update) | async-done | bytes 327696 | tf_op jit(solution)/shard_map/reduce_scatter | solution.py:71
  176.6 46.0 %reduce-scatter.8.cloned.1.call-done = bf16[160,1024]{1,0:T(8,128)(2,1)} async-done(((bf16[1280,1024]{1,0:T(8,128)(2,1)}), bf16[160,1024]{1,0:T(8,128)(2,1)}) %reduce-scatter.8.cloned.1.call-update) | async-done | bytes 327696 | tf_op jit(solution)/shard_map/reduce_scatter | solution.py:72
  222.6 2.4 fusion.14
  225.2 0.9 pad_maximum_fusion.1
  226.1 41.8 %all-gather.5.cloned.1.call-done = bf16[1280,1024]{1,0:T(8,128)(2,1)} async-done(((bf16[160,1024]{1,0:T(8,128)(2,1)}), bf16[1280,1024]{1,0:T(8,128)(2,1)}) %all-gather.5.cloned.1.call-update) | async-done | bytes 2621456 | tf_op jit(solution)/shard_map/all_gather | solution.py:80
  267.9 6.8 %fusion.4 = f32[1280,896]{1,0:T(8,128)} fusion(bf16[1280,1024]{1,0:T(8,128)(2,1)} %all-gather.5.cloned.1.call-done, bf16[1,896,1024]{2,1,0:T(8,128)(2,1)S(1)} %copy-done), kind=kOutput, calls=%fused_computation.11 | convolution fusion | flops 2348810240 | bytes 9043968 | tf_op jit(solution)/shard_map/dot_general | solution.py:26
  274.7 61.7 %all-gather.3.cloned.1.call-done = bf16[1280,2048]{1,0:T(8,128)(2,1)} async-done(((bf16[160,2048]{1,0:T(8,128)(2,1)}), bf16[1280,2048]{1,0:T(8,128)(2,1)}) %all-gather.3.cloned.1.call-update) | async-done | bytes 5242896 | tf_op jit(solution)/shard_map/all_gather | solution.py:84
  336.4 8.0 %add_convert_fusion = bf16[1280,896]{1,0:T(8,128)(2,1)} fusion(f32[1280,896]{1,0:T(8,128)} %fusion.4, bf16[1280,2048]{1,0:T(8,128)(2,1)} %all-gather.3.cloned.1.call-done, bf16[1,896,1024]{2,1,0:T(8,128)(2,1)} %param.13), kind=kOutput, calls=%fused_computation | convolution fusion | flops 2351104000 | bytes 11337728 | tf_op jit(solution)/shard_map/dot_general | solution.py:26
  344.4 7.6 %all-to-all-start.4 = ((bf16[32,40,896]{2,1,0:T(8,128)(2,1)}), bf16[32,40,896]{2,1,0:T(8,128)(2,1)}, u32[]{:S(2)}, u32[]{:S(2)}) async-start(bf16[32,40,896]{2,1,0:T(8,128)(2,1)} %bitcast.75), calls=%async_computation.7 | async-start | bytes 4587520 | tf_op jit(solution)/shard_map/all_to_all | solution.py:39
  351.9 6.6 %convolution_convert_fusion.3 = bf16[1280,896]{1,0:T(8,128)(2,1)} fusion(bf16[1280,2048]{1,0:T(8,128)(2,1)} %all-gather.3.cloned.1.call-done, bf16[1,1024,896]{2,1,0:T(8,128)(2,1)} %param.14), kind=kOutput, calls=%fused_computation.4 | convolution fusion | flops 2349957120 | bytes 6750208 | tf_op jit(solution)/shard_map/dot_general | solution.py:107
  358.5 23.9 %all-to-all-done.4 = bf16[32,40,896]{2,1,0:T(8,128)(2,1)} async-done(((bf16[32,40,896]{2,1,0:T(8,128)(2,1)}), bf16[32,40,896]{2,1,0:T(8,128)(2,1)}, u32[]{:S(2)}, u32[]{:S(2)}) %all-to-all-start.4) | async-done | bytes 2293792 | tf_op jit(solution)/shard_map/all_to_all | solution.py:39
  382.4 5.4 %all-to-all-start.3 = ((bf16[32,40,896]{2,1,0:T(8,128)(2,1)}), bf16[32,40,896]{2,1,0:T(8,128)(2,1)}, u32[]{:S(2)}, u32[]{:S(2)}) async-start(bf16[32,40,896]{2,1,0:T(8,128)(2,1)} %bitcast.72), calls=%async_computation.6 | async-start | bytes 4587520 | tf_op jit(solution)/shard_map/all_to_all | solution.py:39
  388.5 2.5 fusion.25
  391.0 1.3 convolution_convert_fusion.6
  392.3 26.1 %all-to-all-done.3 = bf16[32,40,896]{2,1,0:T(8,128)(2,1)} async-done(((bf16[32,40,896]{2,1,0:T(8,128)(2,1)}), bf16[32,40,896]{2,1,0:T(8,128)(2,1)}, u32[]{:S(2)}, u32[]{:S(2)}) %all-to-all-start.3) | async-done | bytes 2293792 | tf_op jit(solution)/shard_map/all_to_all | solution.py:39
  418.4 4.5 %all-to-all-start.5 = ((bf16[32,16,896]{2,1,0:T(8,128)(2,1)}), bf16[32,16,896]{2,1,0:T(8,128)(2,1)S(1)}, u32[]{:S(2)}, u32[]{:S(2)}) async-start(bf16[32,16,896]{2,1,0:T(8,128)(2,1)} %bitcast.23), calls=%async_computation.8 | async-start | bytes 1835008 | tf_op jit(solution)/shard_map/all_to_all | solution.py:39
  422.9 2.5 fusion.26
  426.2 12.3 %all-to-all-done.5 = bf16[32,16,896]{2,1,0:T(8,128)(2,1)S(1)} async-done(((bf16[32,16,896]{2,1,0:T(8,128)(2,1)}), bf16[32,16,896]{2,1,0:T(8,128)(2,1)S(1)}, u32[]{:S(2)}, u32[]{:S(2)}) %all-to-all-start.5) | async-done | bytes 917536 | tf_op jit(solution)/shard_map/all_to_all | solution.py:39
  438.5 1.5 convolution_convert_fusion.8
  (50 shorter events, 6.4 us)
Async XLA Ops:
  7.2 126.2 %copy-start = (bf16[1,896,1024]{2,1,0:T(8,128)(2,1)S(1)}, bf16[1,896,1024]{2,1,0:T(8,128)(2,1)}, u32[]{:S(2)}) copy-start(bf16[1,896,1024]{2,1,0:T(8,128)(2,1)} %param.12) | copy-start | bytes 5505028
  7.2 137.0 %reduce-scatter.4.cloned.1.call-start = ((), (), s32[]{:S(2)}) async-start(), calls=%async_computation.9 | async-start | bytes 2949120 | tf_op jit(solution)/shard_map/reduce_scatter | solution.py:67
  10.3 39.3 %copy-start.4 = (bf16[1,1024,896]{2,1,0:T(8,128)(2,1)S(1)}, bf16[1,1024,896]{2,1,0:T(8,128)(2,1)}, u32[]{:S(2)}) copy-start(bf16[1,1024,896]{2,1,0:T(8,128)(2,1)} %param.14) | copy-start | bytes 5505028
  53.9 0.7 copy-start.6
  53.9 14.9 %copy-start.5 = (bf16[384,896]{1,0:T(8,128)(2,1)S(1)}, bf16[384,896]{1,0:T(8,128)(2,1)}, u32[]{:S(2)}) copy-start(bf16[384,896]{1,0:T(8,128)(2,1)} %param.8) | copy-start | bytes 2064388
  70.5 24.2 %all-to-all-start.1 = ((bf16[32,16,896]{2,1,0:T(8,128)(2,1)}), bf16[32,16,896]{2,1,0:T(8,128)(2,1)S(1)}, u32[]{:S(2)}, u32[]{:S(2)}) async-start(bf16[32,16,896]{2,1,0:T(8,128)(2,1)} %bitcast.78), calls=%async_computation.2 | async-start | bytes 1835008 | tf_op jit(solution)/shard_map/all_to_all | solution.py:39
  79.1 97.5 %reduce-scatter.6.cloned.1.call-start = ((), (), s32[]{:S(2)}) async-start(), calls=%async_computation.10 | async-start | bytes 2949120 | tf_op jit(solution)/shard_map/reduce_scatter | solution.py:71
  131.9 1.5 copy-start.1
  137.5 85.1 %reduce-scatter.8.cloned.1.call-start = ((), (), s32[]{:S(2)}) async-start(), calls=%async_computation.11 | async-start | bytes 2949120 | tf_op jit(solution)/shard_map/reduce_scatter | solution.py:72
  144.1 123.8 %all-gather.5.cloned.1.call-start = ((), (), s32[]{:S(2)}) async-start(), calls=%async_computation.13 | async-start | bytes 2949120 | tf_op jit(solution)/shard_map/all_gather | solution.py:80
  225.0 111.4 %all-gather.3.cloned.1.call-start = ((), (), s32[]{:S(2)}) async-start(), calls=%async_computation.12 | async-start | bytes 5898240 | tf_op jit(solution)/shard_map/all_gather | solution.py:84
  344.4 38.1 %all-to-all-start.4 = ((bf16[32,40,896]{2,1,0:T(8,128)(2,1)}), bf16[32,40,896]{2,1,0:T(8,128)(2,1)}, u32[]{:S(2)}, u32[]{:S(2)}) async-start(bf16[32,40,896]{2,1,0:T(8,128)(2,1)} %bitcast.75), calls=%async_computation.7 | async-start | bytes 4587520 | tf_op jit(solution)/shard_map/all_to_all | solution.py:39
  382.4 5.4 %copy-start.3 = (f32[128,8]{0,1:T(8,128)S(1)}, f32[128,8]{0,1:T(8,128)}, u32[]{:S(2)}) copy-start(f32[128,8]{0,1:T(8,128)} %param.11) | copy-start | bytes 12292
  382.4 5.7 %copy-start.2 = (s32[128,8]{0,1:T(8,128)S(1)}, s32[128,8]{0,1:T(8,128)}, u32[]{:S(2)}) copy-start(s32[128,8]{0,1:T(8,128)} %param.10) | copy-start | bytes 12292
  382.4 36.0 %all-to-all-start.3 = ((bf16[32,40,896]{2,1,0:T(8,128)(2,1)}), bf16[32,40,896]{2,1,0:T(8,128)(2,1)}, u32[]{:S(2)}, u32[]{:S(2)}) async-start(bf16[32,40,896]{2,1,0:T(8,128)(2,1)} %bitcast.72), calls=%async_computation.6 | async-start | bytes 4587520 | tf_op jit(solution)/shard_map/all_to_all | solution.py:39
  418.4 20.1 %all-to-all-start.5 = ((bf16[32,16,896]{2,1,0:T(8,128)(2,1)}), bf16[32,16,896]{2,1,0:T(8,128)(2,1)S(1)}, u32[]{:S(2)}, u32[]{:S(2)}) async-start(bf16[32,16,896]{2,1,0:T(8,128)(2,1)} %bitcast.23), calls=%async_computation.8 | async-start | bytes 1835008 | tf_op jit(solution)/shard_map/all_to_all | solution.py:39
Sparse Core Ops, SparseCore 0:
  54.0 39.0 reduce-scatter.3
  137.6 38.9 reduce-scatter.5
  179.2 43.3 reduce-scatter.7
  225.1 42.8 all-gather.4
  270.1 66.2 all-gather.2
